TPU v7x, 32 devices: a whole 2x2x4 slice. The times are simulated.
32 devices in a mesh: section: 4 (over y, x), tok: 4 (over z), head: 2 (over core).
Axes of the slice: x: 2, y: 2, z: 4, core: 2. Of those that a mesh axis runs over, the one named last changes fastest.
Arguments:
- group_in: bfloat16 [4, 512, 2048], P('section', 'tok'), may hold values from -6 to 6
- w_qkv: bfloat16 [4, 3, 2048, 2048], P('section', None, 'tok', 'head'), may hold values from -0.125 to 0.125
- w_out: bfloat16 [4, 2048, 2048], P('section', 'head', 'tok'), may hold values from -0.125 to 0.125
- step_sizes: float32 [4, 512, 4], P('section', 'tok', 'head'), may hold values from 0.05 to 1
- fast_weights: bfloat16 [4, 4, 3, 512, 512], P('section', 'head'), may hold values from -0.25 to 0.25
- momentum: bfloat16 [4, 4, 3, 512, 512], P('section', 'head'), may hold values from -16 to 16
- momentum_decay: float32 [4, 4], P('section', 'head'), may hold values from 0.5 to 0.95
- fast_rate: float32 [4, 4], P('section', 'head'), may hold values from 0.3 to 1
Outputs:
- handed: bfloat16 [4, 512, 2048], P('section', 'tok', 'head')
- fast_next: bfloat16 [4, 4, 3, 512, 512], P('section', 'head')
All inputs are finite; a program needn't handle non-finite values.
Results may differ from a plain program's by a relative error of at most 0.015.
Values may be sent and summed in bfloat16 or wider, within the bound.
A program may use at most 128 MiB of HBM per device.

v0:
```python
import jax
import jax.numpy as jnp
from jax import lax
from jax.sharding import PartitionSpec as P

NS_ITERS = 2
coef_linear = 3.4445
coef_cubic = -4.775
coef_quintic = 2.0315


def passed_along(value, axis, steps):
    count = lax.axis_size(axis)
    pairs = [(source, (source + steps) % count) for source in range(count)]
    return lax.ppermute(value, axis, pairs)


def rms_rows(values_in, epsilon):
    return values_in * lax.rsqrt(jnp.mean(values_in * values_in, axis=-1, keepdims=True) + epsilon)


def fast_grads(key_rows, value_rows, step_rates, weights):
    gate_pre = jnp.einsum(
        "thi,hij->thj", key_rows, weights[:, 0], preferred_element_type=jnp.float32
    )
    up_pre = jnp.einsum("thi,hij->thj", key_rows, weights[:, 1], preferred_element_type=jnp.float32)
    squash = jax.nn.sigmoid(gate_pre)
    hidden = (gate_pre * squash * up_pre).astype(jnp.bfloat16)
    errors = (-(step_rates[:, :, None] * value_rows.astype(jnp.float32))).astype(jnp.bfloat16)
    back_hidden = jnp.einsum(
        "thi,hij->thj", errors, weights[:, 2], preferred_element_type=jnp.float32
    )
    grad_gate = (back_hidden * up_pre * squash * (1.0 + gate_pre * (1.0 - squash))).astype(
        jnp.bfloat16
    )
    grad_up = (back_hidden * gate_pre * squash).astype(jnp.bfloat16)
    grad_first = jnp.einsum("thi,thj->hij", key_rows, grad_gate, preferred_element_type=jnp.float32)
    grad_third = jnp.einsum("thi,thj->hij", key_rows, grad_up, preferred_element_type=jnp.float32)
    grad_second = jnp.einsum("thi,thj->hij", errors, hidden, preferred_element_type=jnp.float32)
    return jnp.stack([grad_first, grad_third, grad_second], axis=1)


def newton_step(rows_in, gathered):
    gram_matrix = jnp.einsum(
        "mij,mik->mjk", gathered, gathered, preferred_element_type=jnp.float32
    ).astype(jnp.bfloat16)
    cubic_term = jnp.einsum(
        "mij,mjk->mik", rows_in, gram_matrix, preferred_element_type=jnp.float32
    )
    quintic_term = jnp.einsum(
        "mij,mjk->mik",
        cubic_term.astype(jnp.bfloat16),
        gram_matrix,
        preferred_element_type=jnp.float32,
    )
    return (
        coef_linear * rows_in.astype(jnp.float32)
        + coef_cubic * cubic_term
        + coef_quintic * quintic_term
    ).astype(jnp.bfloat16)


def apply_fast(queries, updated):
    gate_pre = jnp.einsum(
        "thi,hij->thj", queries, updated[:, 0], preferred_element_type=jnp.float32
    )
    up_pre = jnp.einsum("thi,hij->thj", queries, updated[:, 1], preferred_element_type=jnp.float32)
    hidden = (jax.nn.silu(gate_pre) * up_pre).astype(jnp.bfloat16)
    output = jnp.einsum("thj,hij->thi", hidden, updated[:, 2], preferred_element_type=jnp.float32)
    return rms_rows(output, 1e-05).astype(jnp.bfloat16)


def shards(group_in, w_qkv, w_out, step_sizes, fast_weights, momentum, momentum_decay, fast_rate):
    tokens = group_in[0]
    tok_rows = tokens.shape[0]
    local_heads = fast_weights.shape[1]
    fan_width = fast_weights.shape[3]
    hid_width = fast_weights.shape[4]
    half_width = w_qkv.shape[3]
    columns = lax.all_to_all(tokens, "tok", split_axis=1, concat_axis=0, tiled=True)
    all_rows = columns.shape[0]
    rates = lax.all_gather(step_sizes[0], "tok", axis=0, tiled=True)
    partial_kv = jnp.einsum(
        "td,jde->jte", columns, w_qkv[0, 1:], preferred_element_type=jnp.float32
    ).astype(jnp.bfloat16)
    partial_q = jnp.dot(columns, w_qkv[0, 0], preferred_element_type=jnp.float32).astype(
        jnp.bfloat16
    )
    summed_kv = lax.psum(partial_kv, "tok").astype(jnp.float32)
    summed_q = lax.psum(partial_q, "tok").astype(jnp.float32)
    shaped = summed_kv.reshape(2, all_rows, local_heads, fan_width)
    key_rows = rms_rows(shaped[0], 1e-06).astype(jnp.bfloat16)
    value_rows = shaped[1].astype(jnp.bfloat16)
    queries = rms_rows(summed_q.reshape(all_rows, local_heads, fan_width), 1e-06).astype(
        jnp.bfloat16
    )
    summed = fast_grads(key_rows, value_rows, rates, fast_weights[0])
    decay_rate = momentum_decay[0][:, None, None, None]
    moment = decay_rate * momentum[0].astype(jnp.float32) + summed
    norm_values = jnp.sqrt(jnp.sum(moment * moment, axis=(2, 3), keepdims=True))
    iterate = (moment / (norm_values + 1e-06)).astype(jnp.bfloat16)
    iterate = iterate.reshape(local_heads * 3, fan_width, hid_width)
    for number in range(NS_ITERS):
        iterate = newton_step(iterate, iterate)
    iterate = iterate.reshape(local_heads, 3, fan_width, hid_width)
    updated = (
        fast_weights[0].astype(jnp.float32)
        - fast_rate[0][:, None, None, None] * iterate.astype(jnp.float32)
    ).astype(jnp.bfloat16)
    mixed_heads = apply_fast(queries, updated).reshape(all_rows, half_width)
    partial_out = jnp.dot(mixed_heads, w_out[0], preferred_element_type=jnp.float32)
    own_rows = lax.all_to_all(
        partial_out.astype(jnp.bfloat16), "tok", split_axis=0, concat_axis=1, tiled=True
    )
    summed_out = lax.psum_scatter(own_rows, "head", scatter_dimension=1, tiled=True).astype(
        jnp.float32
    )
    share_width = summed_out.shape[1]
    own_tokens = lax.dynamic_slice_in_dim(
        tokens, lax.axis_index("head") * share_width, share_width, 1
    )
    layer_out = (own_tokens.astype(jnp.float32) + summed_out).astype(jnp.bfloat16)
    handed = passed_along(layer_out[None], "section", 1)
    return (handed, updated[None])


def solution(mesh):
    placed = (
        P("section", "tok", None),
        P("section", None, "tok", "head"),
        P("section", "head", "tok"),
        P("section", "tok", "head"),
        P("section", "head", None, None, None),
        P("section", "head", None, None, None),
        P("section", "head"),
        P("section", "head"),
    )
    return jax.shard_map(
        shards,
        mesh=mesh,
        in_specs=placed,
        out_specs=(P("section", "tok", "head"), P("section", "head", None, None, None)),
        check_vma=False,
    )
```

profile of v0, /device:TPU:0, one launch (start us, length us, event | category | flops | bytes accessed | tf_op | source)
XLA Modules:
  0.0 256.0 jit_solution(371909318707594207)
XLA Ops:
  7.2 1.5 all_to_all.28
  8.7 0.1 copy.43
  8.9 20.9 %all_to_all.38 = bf16[128,4,512]{2,0,1:T(8,128)(2,1)S(1)} all-to-all(bf16[128,4,512]{2,0,1:T(8,128)(2,1)S(1)} %copy.43), channel_id=1, replica_groups=mesh['section'=4,'tok'=4,'head'=2] {'tok'}, dimensions={1} | all-to-all | bytes 1048576 | tf_op jit(solution)/shard_map/all_to_all | solution.py:80
  29.8 1.9 convolution_convert_fusion.2
  31.7 1.1 copy.83
  32.8 2.7 %convert_bitcast_fusion = bf16[2,512,1024]{1,2,0:T(8,128)(2,1)} fusion(bf16[512,512,1]{1,0,2:T(8,128)(2,1)S(1)} %bitcast.205, bf16[1,3,512,1024]{3,2,1,0:T(8,128)(2,1)S(1)} %copy-done.10), kind=kOutput, calls=%fused_computation.64 | convolution fusion | flops 1074790400 | bytes 4718592 | tf_op jit(solution)/shard_map/td,jde->jte/dot_general | solution.py:83
  35.5 3.9 %copy.82 = bf16[1,2,3,512,512]{4,3,1,2,0:T(8,128)(2,1)} copy(bf16[1,2,3,512,512]{4,3,2,1,0:T(8,128)(2,1)} %param.12) | data formatting | bytes 6291456 | tf_op args[4]
  39.5 0.1 mul.145
  39.6 3.1 %copy_convert_fusion = f32[1,2,3,512,512]{4,3,1,2,0:T(8,128)S(1)} fusion(bf16[1,2,3,512,512]{4,3,2,1,0:T(8,128)(2,1)} %param.13), kind=kLoop, calls=%fused_computation.16 | loop fusion | flops 1572864 | bytes 9437184 | tf_op jit(solution)/shard_map/convert_element_type | solution.py:99
  42.8 3.4 %copy.41 = f32[1,2,3,512,512]{4,3,2,1,0:T(8,128)} copy(f32[1,2,3,512,512]{4,3,1,2,0:T(8,128)S(1)} %copy_convert_fusion) | data formatting | bytes 12582912 | tf_op jit(solution)/shard_map/convert_element_type | solution.py:99
  46.1 9.2 %all-gather = f32[1,512,2]{1,2,0:T(2,128)S(1)} all-gather(f32[1,128,2]{1,2,0:T(2,128)S(1)} %copy-done.8), channel_id=2, replica_groups=mesh['section'=4,'tok'=4,'head'=2] {'tok'}, dimensions={1}, use_global_device_ids=true | all-gather | bytes 5120 | tf_op jit(solution)/shard_map/all_gather | solution.py:82
  55.3 100.5 %all-reduce.3.cloned.1.call-done = (bf16[2,512,1024]{1,2,0:T(8,128)(2,1)}, bf16[512,2,512]{2,0,1:T(8,128)(2,1)}) async-done(((bf16[2,512,1024]{1,2,0:T(8,128)(2,1)}, bf16[512,2,512]{2,0,1:T(8,128)(2,1)}), (bf16[2,512,1024]{1,2,0:T(8,128)(2,1)}, bf16[512,2,512]{2,0,1:T(8,128)(2,1)})) %all-reduce.3.cloned.1.call-update) | async-done | bytes 3145744 | tf_op jit(solution)/shard_map/psum | solution.py:89
  155.8 1.8 fusion.71
  157.7 0.2 fusion.18
  157.9 0.4 copy-done.3
  158.3 0.8 fusion.46
  159.1 0.8 fusion.47
  159.9 0.8 fusion.48
  160.6 1.0 convolution_bitcast_fusion.1
  161.6 1.3 convolution_bitcast_fusion.2
  162.9 1.0 convolution_bitcast_fusion
  163.9 0.9 copy-done.2
  164.8 2.1 fusion.2
  166.9 3.4 %copy.47 = f32[2,3,512,512]{3,2,1,0:T(8,128)} copy(f32[2,3,512,512]{3,2,0,1:T(8,128)S(1)} %get-tuple-element.5) | data formatting | bytes 12582912 | tf_op jit(solution)/shard_map/stack | solution.py:40
  170.2 0.1 copy.48
  170.3 0.1 add.85
  170.4 6.4 %fusion.4 = bf16[6,512,512]{2,1,0:T(8,128)(2,1)S(1)} fusion(f32[2,3,512,512]{3,2,1,0:T(8,128)} %copy.47, f32[1,2,3,512,512]{4,3,2,1,0:T(8,128)} %copy.41, f32[6]{0:T(128)S(1)} %add.85, f32[6]{0:T(128)S(1)} %mul.145), kind=kLoop, calls=%fused_computation.7 | loop fusion | flops 6291456 | bytes 15728688 | tf_op jit(solution)/shard_map/convert_element_type | solution.py:101
  176.8 1.8 convolution_convert_fusion.1
  178.6 4.5 %fusion.74 = f32[6,512,512]{2,1,0:T(8,128)} fusion(bf16[6,512,512]{2,1,0:T(8,128)(2,1)S(1)} %fusion.4, bf16[6,512,512]{2,1,0:T(8,128)(2,1)S(1)} %convolution_convert_fusion.1), kind=kOutput, calls=%fused_computation.99 | convolution fusion | flops 1610612736 | bytes 12582912 | tf_op jit(solution)/shard_map/mij,mjk->mik/dot_general | solution.py:47
  183.1 6.9 %add_convert_fusion.1 = bf16[6,512,512]{2,1,0:T(8,128)(2,1)S(1)} fusion(f32[6,512,512]{2,1,0:T(8,128)} %fusion.74, bf16[6,512,512]{2,1,0:T(8,128)(2,1)S(1)} %fusion.4, bf16[6,512,512]{2,1,0:T(8,128)(2,1)S(1)} %convolution_convert_fusion.1), kind=kOutput, calls=%fused_computation.14 | convolution fusion | flops 1623195648 | bytes 15728640 | tf_op jit(solution)/shard_map/mij,mjk->mik/dot_general | solution.py:50
  189.9 1.8 convolution_convert_fusion
  191.8 1.8 fusion.75
  193.6 2.4 fusion.7
  196.1 0.3 fusion.16
  196.4 5.0 %fusion.6 = bf16[2,3,512,512]{3,2,0,1:T(8,128)(2,1)S(1)} fusion(f32[2,3,512,512]{3,2,1,0:T(8,128)S(1)} %bitcast.187, f32[2]{0:T(128)S(1)} %bitcast.209, bf16[1,2,3,512,512]{4,3,2,1,0:T(8,128)(2,1)} %param.12), kind=kLoop, calls=%fused_computation.11 | loop fusion | flops 6291456 | bytes 12582920 | tf_op jit(solution)/shard_map/convert_element_type | solution.py:109
  201.4 1.7 copy-done.4
  203.1 2.1 fusion.45
  205.2 5.1 %fusion.24 = (f32[512,2]{0,1:T(2,128)S(1)}, f32[2,512,512]{2,1,0:T(8,128)}) fusion(f32[2,512,512]{1,2,0:T(8,128)} %fusion.45, bf16[2,3,512,512]{3,2,0,1:T(8,128)(2,1)} %copy-done.4, bf16[512,2,512]{2,0,1:T(8,128)(2,1)S(1)} %copy-done.5, f32[512,2]{0,1:T(2,128)S(1)} %add_rsqrt_fusion.1), kind=kOutput, calls=%fused_computation.39 | convolution fusion | flops 1079507968 | bytes 7348224 | tf_op jit(solution)/shard_map/thj,hij->thi/dot_general | solution.py:69
  210.3 1.9 fusion.25
  212.2 0.7 convolution_convert_fusion.3
  213.0 17.0 %all_to_all.39 = bf16[4,128,512]{2,1,0:T(8,128)(2,1)S(1)} all-to-all(bf16[4,128,512]{2,1,0:T(8,128)(2,1)S(1)} %bitcast.206), channel_id=1, replica_groups=mesh['section'=4,'tok'=4,'head'=2] {'tok'}, dimensions={0} | all-to-all | bytes 1048576 | tf_op jit(solution)/shard_map/all_to_all | solution.py:112
  230.0 0.8 copy.69
  230.9 7.2 %reduce-scatter.2.cloned.1.call-done = bf16[128,1024]{1,0:T(8,128)(2,1)} async-done(((bf16[128,2048]{1,0:T(8,128)(2,1)}), bf16[128,1024]{1,0:T(8,128)(2,1)}) %reduce-scatter.2.cloned.1.call-update) | async-done | bytes 262160 | tf_op jit(solution)/shard_map/reduce_scatter | solution.py:115
  238.0 1.0 fusion.66
  239.0 1.7 collective-permute-start
  240.8 6.5 %subtract_convert_fusion = bf16[1,2,3,512,512]{4,3,2,1,0:T(8,128)(2,1)} fusion(f32[1,2,3,512,512]{4,3,2,1,0:T(8,128)} %bitcast.188, bf16[1,2,3,512,512]{4,3,2,1,0:T(8,128)(2,1)} %param.12, f32[2]{0:T(128)S(1)} %bitcast.210), kind=kLoop, calls=%fused_computation.12 | loop fusion | flops 6291456 | bytes 12582920 | tf_op jit(solution)/shard_map/convert_element_type | solution.py:109
  247.2 1.3 collective-permute-done
  248.5 0.7 copy.87
  (28 shorter events, 0.3 us)
Async XLA Ops:
  7.2 205.0 %copy-start = (bf16[1,1024,512]{2,1,0:T(8,128)(2,1)S(1)}, bf16[1,1024,512]{2,1,0:T(8,128)(2,1)}, u32[]{:S(2)}) copy-start(bf16[1,1024,512]{2,1,0:T(8,128)(2,1)} %param.10) | copy-start | bytes 3145732
  7.2 148.6 %all-reduce.3.cloned.1.call-start = ((), (), s32[]{:S(2)}) async-start(), calls=%async_computation.4 | async-start | bytes 6291456 | tf_op jit(solution)/shard_map/psum | solution.py:89
  8.8 23.9 %copy-start.10 = (bf16[1,3,512,1024]{3,2,1,0:T(8,128)(2,1)S(1)}, bf16[1,3,512,1024]{3,2,1,0:T(8,128)(2,1)}, u32[]{:S(2)}) copy-start(bf16[1,3,512,1024]{3,2,1,0:T(8,128)(2,1)} %param.9) | copy-start | bytes 9437188
  35.5 4.0 %copy-start.9 = (f32[1,2]{1,0:T(1,128)S(1)}, f32[1,2]{1,0:T(1,128)}, u32[]{:S(2)}) copy-start(f32[1,2]{1,0:T(1,128)} %param.14) | copy-start | bytes 28
  35.5 202.5 %reduce-scatter.2.cloned.1.call-start = ((), (), s32[]{:S(2)}) async-start(), calls=%async_computation.3 | async-start | bytes 786432 | tf_op jit(solution)/shard_map/reduce_scatter | solution.py:115
  42.8 3.4 %copy-start.8 = (f32[1,128,2]{1,2,0:T(2,128)S(1)}, f32[1,128,2]{1,2,0:T(2,128)}, u32[]{:S(2)}) copy-start(f32[1,128,2]{1,2,0:T(2,128)} %param.11) | copy-start | bytes 3076
  155.8 2.5 copy-start.3
  162.9 1.9 copy-start.2
  193.6 2.5 copy-start.5
  193.6 2.8 %copy-start.7 = (f32[1,2]{1,0:T(1,128)S(1)}, f32[1,2]{1,0:T(1,128)}, u32[]{:S(2)}) copy-start(f32[1,2]{1,0:T(1,128)} %param.15) | copy-start | bytes 28
  196.1 5.4 %copy-start.1 = (f32[6,512,512]{2,1,0:T(8,128)}, f32[6,512,512]{2,1,0:T(8,128)S(1)}, u32[]{:S(2)}) copy-start(f32[6,512,512]{2,1,0:T(8,128)S(1)} %fusion.7) | copy-start | bytes 18874372
  201.4 1.7 copy-start.4
  212.2 25.8 %copy-start.6 = (bf16[1,128,2048]{2,1,0:T(8,128)(2,1)S(1)}, bf16[1,128,2048]{2,1,0:T(8,128)(2,1)}, u32[]{:S(2)}) copy-start(bf16[1,128,2048]{2,1,0:T(8,128)(2,1)} %param.8) | copy-start | bytes 1572868
  239.0 9.5 %collective-permute-start = (bf16[1,128,1024]{2,1,0:T(8,128)(2,1)S(1)}, bf16[1,128,1024]{2,1,0:T(8,128)(2,1)S(1)}, u32[]{:S(2)}, u32[]{:S(2)}) collective-permute-start(bf16[1,128,1024]{2,1,0:T(8,128)(2,1)S(1)} %fusion.66), channel_id=1, source_target_pairs={{0,8},{8,16},{16,24},{24,0},{1,9},{9,17},{17,25},{25,1},{2,10},{10... | collective-permute-start | bytes 786440 | tf_op jit(solution)/shard_map/ppermute | solution.py:15
Sparse Core Ops, SparseCore 0:
  35.6 120.1 all-reduce.2
  231.0 6.9 reduce-scatter.1
where the time goes:
time: 257 us; the launch traced here: 256 us
  waiting for transfers between devices  109 us (42%)
  blocking collectives  47.1 us (18%)
  matrix products  37.3 us (15%)
  other arithmetic  26.5 us (10%)
  local copies, waits for them, and re-layouts  20.1 us (8%)
  between operations  14.3 us (6%)
    psum x1, waiting for transfers between devices, shards(): summed_kv = lax.psum(partial_kv, 'tok').astype(jnp.float32)  101 us
    all_to_all x1, blocking collectives, shards(): lax.all_to_all(tokens, 'tok', split_axis=1, concat_axis=0, tiled=True)  20.9 us
    all_to_all x1, blocking collectives, shards(): lax.all_to_all(partial_out.astype(jnp.bfloat16), 'tok', split_axis=0, con...  17 us
    convert_element_type x2, other arithmetic, shards(): updated = (fast_weights[0].astype(jnp.float32) - fast_rate[0][:, None, No...  11.5 us
    dot_general x2, matrix products, newton_step(): jnp.einsum('mij,mjk->mik', cubic_term.astype(jnp.bfloat16), gram_matrix,...  9.3 us
    all_gather x1, blocking collectives, shards(): rates = lax.all_gather(step_sizes[0], 'tok', axis=0, tiled=True)  9.16 us
    unnamed x24, local copies, waits for them, and re-layouts  7.67 us
    reduce_scatter x1, waiting for transfers between devices, shards(): lax.psum_scatter(own_rows, 'head', scatter_dimension=1, tiled=True)  7.15 us
  transfers between devices with their start and end apart: 3, of which 3 were waited for; matrix products, arithmetic and copies ran while one was open for 7% of the time, Pallas kernels for 0%

commit v1 on v0

--- a/solution.py
+++ b/solution.py
@@ -7,6 +7,11 @@
 coef_linear = 3.4445
 coef_cubic = -4.775
 coef_quintic = 2.0315
+
+
+def summed_here(block, axis):
+    parts = lax.all_gather(block, axis)
+    return jnp.sum(parts, axis=0)
 
 
 def passed_along(value, axis, steps):
@@ -86,7 +91,7 @@
     partial_q = jnp.dot(columns, w_qkv[0, 0], preferred_element_type=jnp.float32).astype(
         jnp.bfloat16
     )
-    summed_kv = lax.psum(partial_kv, "tok").astype(jnp.float32)
+    summed_kv = summed_here(partial_kv, "tok").astype(jnp.float32)
     summed_q = lax.psum(partial_q, "tok").astype(jnp.float32)
     shaped = summed_kv.reshape(2, all_rows, local_heads, fan_width)
     key_rows = rms_rows(shaped[0], 1e-06).astype(jnp.bfloat16)

time: 257 us -> 356 us (1.39)
  waiting for transfers between devices: 109 us -> 183 us
  other arithmetic: 26.5 us -> 38.4 us
  local copies, waits for them, and re-layouts: 20.1 us -> 28.3 us
  matrix products: 37.3 us -> 42.4 us
    all_gather x0 -> x1, waiting for transfers between devices: none -> 149 us  [summed_here(): parts = lax.all_gather(block, axis)]
    psum x1, waiting for transfers between devices: 101 us -> 25.8 us  [shards(): summed_q = lax.psum(partial_q, 'tok').astype(jnp.float32)]
    reduce_sum x0 -> x1, other arithmetic: none -> 6.31 us  [summed_here(): return jnp.sum(parts, axis=0)]
    convert_element_type x0 -> x2, local copies, waits for them, and re-layouts: none -> 5.36 us  [the longest x1 2.92 us: fast_grads(): value_rows.astype(jnp.float32)]
    convert_element_type x0 -> x2, other arithmetic: none -> 4.35 us  [the longest x1 2.41 us: fast_grads(): value_rows.astype(jnp.float32)]
    squeeze x0 -> x2, local copies, waits for them, and re-layouts: none -> 3.75 us  [shards(): key_rows = rms_rows(shaped[0], 1e-06).astype(jnp.bfloat16)]
    unnamed x24 -> x30, local copies, waits for them, and re-layouts: 7.67 us -> 8.54 us
  transfers between devices with their start and end apart: 3 -> 4, of which waited for: 3 -> 4; matrix products, arithmetic and copies ran while one was open for 7% -> 7% of each run, Pallas kernels for 0% -> 0%
where the time goes in v1:
time: 356 us
  waiting for transfers between devices  183 us (51%)
  blocking collectives  47.5 us (13%)
  matrix products  42.4 us (12%)
  other arithmetic  38.4 us (11%)
  local copies, waits for them, and re-layouts  28.3 us (8%)
  between operations  14 us (4%)
    all_gather x1, waiting for transfers between devices, summed_here(): parts = lax.all_gather(block, axis)  149 us
    psum x1, waiting for transfers between devices, shards(): summed_q = lax.psum(partial_q, 'tok').astype(jnp.float32)  25.8 us
    all_to_all x1, blocking collectives, shards(): lax.all_to_all(tokens, 'tok', split_axis=1, concat_axis=0, tiled=True)  20.6 us
    all_to_all x1, blocking collectives, shards(): lax.all_to_all(partial_out.astype(jnp.bfloat16), 'tok', split_axis=0, con...  17.3 us
    convert_element_type x2, other arithmetic, shards(): updated = (fast_weights[0].astype(jnp.float32) - fast_rate[0][:, None, No...  11.9 us
    all_gather x1, blocking collectives, shards(): rates = lax.all_gather(step_sizes[0], 'tok', axis=0, tiled=True)  9.55 us
    dot_general x2, matrix products, newton_step(): jnp.einsum('mij,mjk->mik', cubic_term.astype(jnp.bfloat16), gram_matrix,...  9.35 us
    unnamed x30, local copies, waits for them, and re-layouts  8.54 us
  transfers between devices with their start and end apart: 4, of which 4 were waited for; matrix products, arithmetic and copies ran while one was open for 7% of the time, Pallas kernels for 0%

profile of v1, /device:TPU:0, one launch (start us, length us, event | category | flops | bytes accessed | tf_op | source)
XLA Modules:
  0.0 355.7 jit_solution(16210271070615239816)
XLA Ops:
  7.2 1.5 all_to_all.28
  8.8 20.6 %all_to_all.38 = bf16[128,4,512]{2,0,1:T(8,128)(2,1)S(1)} all-to-all(bf16[128,4,512]{2,0,1:T(8,128)(2,1)S(1)} %copy.160), channel_id=1, replica_groups=mesh['section'=4,'tok'=4,'head'=2] {'tok'}, dimensions={1} | all-to-all | bytes 1048576 | tf_op jit(solution)/shard_map/all_to_all | solution.py:85
  29.5 2.1 convolution_convert_fusion.2
  31.6 1.1 copy.208
  32.8 3.0 convert_bitcast_fusion
  35.8 2.4 copy.161
  38.3 3.9 %copy.207 = bf16[1,2,3,512,512]{4,3,1,2,0:T(8,128)(2,1)} copy(bf16[1,2,3,512,512]{4,3,2,1,0:T(8,128)(2,1)} %param.12) | data formatting | bytes 6291456 | tf_op args[4]
  42.4 2.8 copy_convert_fusion
  45.2 3.4 copy.158
  48.6 9.5 %all-gather.1 = f32[1,512,2]{1,2,0:T(2,128)S(1)} all-gather(f32[1,128,2]{1,2,0:T(2,128)S(1)} %copy-done.12), channel_id=3, replica_groups=mesh['section'=4,'tok'=4,'head'=2] {'tok'}, dimensions={1}, use_global_device_ids=true | all-gather | bytes 5120 | tf_op jit(solution)/shard_map/all_gather | solution.py:87
  58.2 25.8 %all-reduce.2.cloned.1.call-done = bf16[512,2,512]{2,0,1:T(8,128)(2,1)} async-done(((bf16[512,2,512]{2,0,1:T(8,128)(2,1)}), bf16[512,2,512]{2,0,1:T(8,128)(2,1)}) %all-reduce.2.cloned.1.call-update) | async-done | bytes 1048592 | tf_op jit(solution)/shard_map/psum | solution.py:95
  84.0 1.5 fusion.16
  85.5 149.0 %all-gather.4.cloned.1.call-done = bf16[8,512,1024]{2,1,0:T(8,128)(2,1)} async-done(((bf16[2,512,1024]{2,1,0:T(8,128)(2,1)}), bf16[8,512,1024]{2,1,0:T(8,128)(2,1)}) %all-gather.4.cloned.1.call-update) | async-done | bytes 8388624 | tf_op jit(solution)/shard_map/all_gather | solution.py:13
  234.4 6.3 %reduce_sum.48 = bf16[2,512,1024]{2,1,0:T(8,128)(2,1)S(1)} reduce(bf16[4,2,512,1024]{3,2,1,0:T(8,128)(2,1)} %bitcast.197, bf16[]{:T(256)} %constant.9.clone.1), dimensions={0}, to_apply=%region_0.0 | reduce | flops 3145728 | bytes 10485762 | tf_op jit(solution)/shard_map/reduce_sum | solution.py:14
  240.8 2.4 slice_convert_fusion
  243.2 1.9 copy.162
  245.1 1.8 copy.165
  247.2 1.9 multiply_convert_fusion
  249.5 2.0 fusion.42
  251.5 2.0 fusion.43
  253.5 2.9 copy.190
  256.4 2.8 fusion.44
  259.2 1.0 convolution_bitcast_fusion.1
  260.8 1.3 convolution_bitcast_fusion.2
  262.4 0.9 convolution_bitcast_fusion
  263.3 0.9 copy-done.2
  264.3 2.2 fusion.2
  266.5 3.4 copy.170
  270.0 6.4 %fusion.4 = bf16[6,512,512]{2,1,0:T(8,128)(2,1)S(1)} fusion(f32[2,3,512,512]{3,2,1,0:T(8,128)} %copy.170, f32[1,2,3,512,512]{4,3,2,1,0:T(8,128)} %copy.158, f32[6]{0:T(128)S(1)} %add.83, f32[6]{0:T(128)S(1)} %mul.145), kind=kLoop, calls=%fused_computation.7 | loop fusion | flops 6291456 | bytes 15728688 | tf_op jit(solution)/shard_map/convert_element_type | solution.py:106
  276.4 1.8 convolution_convert_fusion.1
  278.2 4.5 %fusion.63 = f32[6,512,512]{2,1,0:T(8,128)} fusion(bf16[6,512,512]{2,1,0:T(8,128)(2,1)S(1)} %fusion.4, bf16[6,512,512]{2,1,0:T(8,128)(2,1)S(1)} %convolution_convert_fusion.1), kind=kOutput, calls=%fused_computation.96 | convolution fusion | flops 1610612736 | bytes 12582912 | tf_op jit(solution)/shard_map/mij,mjk->mik/dot_general | solution.py:52
  282.7 6.9 %add_convert_fusion.1 = bf16[6,512,512]{2,1,0:T(8,128)(2,1)S(1)} fusion(f32[6,512,512]{2,1,0:T(8,128)} %fusion.63, bf16[6,512,512]{2,1,0:T(8,128)(2,1)S(1)} %fusion.4, bf16[6,512,512]{2,1,0:T(8,128)(2,1)S(1)} %convolution_convert_fusion.1), kind=kOutput, calls=%fused_computation.14 | convolution fusion | flops 1623195648 | bytes 15728640 | tf_op jit(solution)/shard_map/mij,mjk->mik/dot_general | solution.py:55
  289.6 1.8 convolution_convert_fusion
  291.4 1.8 fusion.64
  293.2 2.5 fusion.7
  295.7 5.4 %fusion.6 = bf16[2,3,512,512]{3,2,0,1:T(8,128)(2,1)S(1)} fusion(f32[2,3,512,512]{3,2,1,0:T(8,128)S(1)} %bitcast.190, f32[2]{0:T(128)S(1)} %bitcast.210, bf16[1,2,3,512,512]{4,3,2,1,0:T(8,128)(2,1)} %param.12), kind=kLoop, calls=%fused_computation.11 | loop fusion | flops 6291456 | bytes 12582920 | tf_op jit(solution)/shard_map/convert_element_type | solution.py:114
  301.1 1.7 copy-done.5
  302.8 2.1 fusion.41
  304.9 5.1 %fusion.20 = (f32[512,2]{0,1:T(2,128)S(1)}, f32[2,512,512]{2,1,0:T(8,128)}) fusion(f32[2,512,512]{1,2,0:T(8,128)} %fusion.41, bf16[2,3,512,512]{3,2,0,1:T(8,128)(2,1)} %copy-done.5, bf16[512,2,512]{2,0,1:T(8,128)(2,1)S(1)} %copy-done.6, f32[512,2]{0,1:T(2,128)S(1)} %add_rsqrt_fusion.1), kind=kOutput, calls=%fused_computation.32 | convolution fusion | flops 1079507968 | bytes 7348224 | tf_op jit(solution)/shard_map/thj,hij->thi/dot_general | solution.py:74
  310.0 1.9 fusion.21
  311.9 0.7 convolution_convert_fusion.3
  312.7 17.3 %all_to_all.39 = bf16[4,128,512]{2,1,0:T(8,128)(2,1)S(1)} all-to-all(bf16[4,128,512]{2,1,0:T(8,128)(2,1)S(1)} %bitcast.207), channel_id=1, replica_groups=mesh['section'=4,'tok'=4,'head'=2] {'tok'}, dimensions={0} | all-to-all | bytes 1048576 | tf_op jit(solution)/shard_map/all_to_all | solution.py:117
  330.0 0.8 copy.194
  330.9 7.1 %reduce-scatter.2.cloned.1.call-done = bf16[128,1024]{1,0:T(8,128)(2,1)} async-done(((bf16[128,2048]{1,0:T(8,128)(2,1)}), bf16[128,1024]{1,0:T(8,128)(2,1)}) %reduce-scatter.2.cloned.1.call-update) | async-done | bytes 262160 | tf_op jit(solution)/shard_map/reduce_scatter | solution.py:120
  338.0 1.0 fusion.56
  339.0 1.7 collective-permute-start
  340.7 6.5 %subtract_convert_fusion = bf16[1,2,3,512,512]{4,3,2,1,0:T(8,128)(2,1)} fusion(f32[1,2,3,512,512]{4,3,2,1,0:T(8,128)} %bitcast.191, bf16[1,2,3,512,512]{4,3,2,1,0:T(8,128)(2,1)} %param.12, f32[2]{0:T(128)S(1)} %bitcast.211), kind=kLoop, calls=%fused_computation.12 | loop fusion | flops 6291456 | bytes 12582920 | tf_op jit(solution)/shard_map/convert_element_type | solution.py:114
  347.2 1.2 collective-permute-done
  (43 shorter events, 2.8 us)
Async XLA Ops:
  7.2 304.7 %copy-start = (bf16[1,1024,512]{2,1,0:T(8,128)(2,1)S(1)}, bf16[1,1024,512]{2,1,0:T(8,128)(2,1)}, u32[]{:S(2)}) copy-start(bf16[1,1024,512]{2,1,0:T(8,128)(2,1)} %param.10) | copy-start | bytes 3145732
  7.2 76.8 %all-reduce.2.cloned.1.call-start = ((), (), s32[]{:S(2)}) async-start(), calls=%async_computation.3 | async-start | bytes 2097152 | tf_op jit(solution)/shard_map/psum | solution.py:95
  29.5 3.3 copy-start.10
  32.8 201.7 %all-gather.4.cloned.1.call-start = ((), (), s32[]{:S(2)}) async-start(), calls=%async_computation.5 | async-start | bytes 10485760 | tf_op jit(solution)/shard_map/all_gather | solution.py:13
  38.3 4.0 %copy-start.13 = (f32[1,2]{1,0:T(1,128)S(1)}, f32[1,2]{1,0:T(1,128)}, u32[]{:S(2)}) copy-start(f32[1,2]{1,0:T(1,128)} %param.14) | copy-start | bytes 28
  38.3 299.7 %reduce-scatter.2.cloned.1.call-start = ((), (), s32[]{:S(2)}) async-start(), calls=%async_computation.4 | async-start | bytes 786432 | tf_op jit(solution)/shard_map/reduce_scatter | solution.py:120
  45.2 3.4 copy-start.12
  246.9 2.5 copy-start.3
  256.4 2.8 copy-start.7
  259.2 1.6 copy-start.8
  260.8 1.6 copy-start.4
  262.4 1.9 copy-start.2
  293.2 2.5 copy-start.11
  295.7 5.4 %copy-start.1 = (f32[6,512,512]{2,1,0:T(8,128)}, f32[6,512,512]{2,1,0:T(8,128)S(1)}, u32[]{:S(2)}) copy-start(f32[6,512,512]{2,1,0:T(8,128)S(1)} %fusion.7) | copy-start | bytes 18874372
  295.7 7.1 %copy-start.6 = (bf16[512,2,512]{2,0,1:T(8,128)(2,1)S(1)}, bf16[512,2,512]{2,0,1:T(8,128)(2,1)}, u32[]{:S(2)}) copy-start(bf16[512,2,512]{2,0,1:T(8,128)(2,1)} %all-reduce.2.cloned.1.call-done) | copy-start | bytes 3145732
  301.1 1.7 copy-start.5
  311.9 26.1 %copy-start.9 = (bf16[1,128,2048]{2,1,0:T(8,128)(2,1)S(1)}, bf16[1,128,2048]{2,1,0:T(8,128)(2,1)}, u32[]{:S(2)}) copy-start(bf16[1,128,2048]{2,1,0:T(8,128)(2,1)} %param.8) | copy-start | bytes 1572868
  339.0 9.5 %collective-permute-start = (bf16[1,128,1024]{2,1,0:T(8,128)(2,1)S(1)}, bf16[1,128,1024]{2,1,0:T(8,128)(2,1)S(1)}, u32[]{:S(2)}, u32[]{:S(2)}) collective-permute-start(bf16[1,128,1024]{2,1,0:T(8,128)(2,1)S(1)} %fusion.56), channel_id=1, source_target_pairs={{0,8},{8,16},{16,24},{24,0},{1,9},{9,17},{17,25},{25,1},{2,10},{10... | collective-permute-start | bytes 786440 | tf_op jit(solution)/shard_map/ppermute | solution.py:20
Sparse Core Ops, SparseCore 0:
  32.9 51.0 all-reduce.1
  85.5 148.8 all-gather.3
  331.0 6.9 reduce-scatter.1
